TPU v7x, 32 devices: a whole 2x2x4 slice. The times are simulated.
32 devices in a mesh: ens: 2 (over y), lon: 4 (over x, core), lat: 4 (over z).
Axes of the slice: x: 2, y: 2, z: 4, core: 2. Of those that a mesh axis runs over, the one named last changes fastest.
Arguments:
- noise: float32 [64, 64, 512], P('ens', 'lat', 'lon'), parts along dimension 0, may hold values from -6 to 6
- kappa2: float32 [32, 64, 512], P(None, 'lat', 'lon'), may hold values from 0.03 to 0.3
- conduct: float32 [3, 32, 64, 512], P(None, None, 'lat', 'lon'), may hold values from 0.3 to 3
- land: int32 [32, 64, 512], P(None, 'lat', 'lon'), may hold values 0 or 1
Outputs:
- solution_field: float32 [64, 64, 512], P('ens', 'lat', 'lon'), parts along dimension 0
- residual: float32 [64, 64, 512], P('ens', 'lat', 'lon'), parts along dimension 0
There are 2 independent parts, one for each index of `ens`. A program takes and returns all parts, laid end to end along the dimension named above; an argument that names none is the same for every part. Nothing has to cross between parts.
Inputs may be any that keep to these rules, and one draw needn't show every extreme that they name: 1 marks an ocean cell, 0 a land cell.
All inputs are finite; a program needn't handle non-finite values. No bound on the sum of `land` on one device may be relied on, other than what follows from the above.
Results may differ from a plain program's by a relative error of at most 0.00035.
Values sent between devices are 32-bit elements; how exact they have to be, the bound alone decides.
No kernel may reach another device: no remote copies, remote signals or barrier semaphores. Data moves between devices by JAX's collectives and lax.ppermute only.
A program may use at most 64 MiB of HBM per device.

v0:
```python
import math
import jax
import jax.numpy as jnp
from jax import lax
from jax.sharding import PartitionSpec as P

ITERS = 2
base_kappa = 0.001
base_conduct = 1.0


def padded_2(x, sides, width, wrap):
    for axis, dim in sides:
        size, length = (lax.axis_size(axis), x.shape[dim])
        up = [(i, (i + 1) % size) for i in range(size if wrap else size - 1)]
        down = [(j, i) for i, j in up]
        last = lax.slice_in_dim(x, length - width, length, axis=dim)
        initial = lax.slice_in_dim(x, 0, width, axis=dim)
        before = lax.ppermute(last, axis, up)
        after = lax.ppermute(initial, axis, down)
        x = jnp.concatenate([before, x, after], axis=dim)
    return x


def shifted(x, axis, by):
    size = lax.axis_size(axis)
    return lax.ppermute(x, axis, [(i, (i + by) % size) for i in range(size)])


def shifted_2(x, axis, by):
    size = lax.axis_size(axis)
    pairs = [(i, i + by) for i in range(size) if 0 <= i + by < size]
    return lax.ppermute(x, axis, pairs)


def cut_cycle(padded, width, extend):
    margin = width - extend
    return padded[:, :, margin : padded.shape[2] - margin, margin : padded.shape[3] - margin]


def divergence_form(padded, statics, width, extend):
    cycle = cut_cycle(statics, width, extend + 1)
    kappa_cells = cycle[0][:, 1:-1, 1:-1]
    east_face = cycle[2][:, 1:-1, 1:-1]
    west_face = cycle[2][:, 1:-1, :-2]
    north_face = cycle[3][:, 1:-1, 1:-1]
    south_face = cycle[3][:, :-2, 1:-1]
    upper_face = cycle[4][:, 1:-1, 1:-1]
    center = padded[:, 1:-1, 1:-1]
    zero_level = jnp.zeros_like(center[:1])
    lower_face = jnp.concatenate([zero_level, upper_face[:-1]], axis=0)
    upper_value = jnp.concatenate([center[1:], zero_level], axis=0)
    lower_value = jnp.concatenate([zero_level, center[:-1]], axis=0)
    return (
        kappa_cells * center
        + east_face * (center - padded[:, 1:-1, 2:])
        + west_face * (center - padded[:, 1:-1, :-2])
        + north_face * (center - padded[:, 2:, 1:-1])
        + south_face * (center - padded[:, :-2, 1:-1])
        + upper_face * (center - upper_value)
        + lower_face * (center - lower_value)
    )


def pad_each(field):
    across = padded_2(field, (("lon", 2),), 1, True)
    return padded_2(across, (("lat", 1),), 1, False)


def operator(field, statics, width):
    ocean = cut_cycle(statics, width, 0)[1]
    first = divergence_form(pad_each(ocean * field), statics, width, 0)
    second = divergence_form(pad_each(ocean * first), statics, width, 0)
    return ocean * second + (1.0 - ocean) * field


def spectral(block, width):
    length = block.shape[2]
    count_a = length // width
    lead = block.shape[:2]
    shaped = block.reshape(lead + (count_a, width))
    index_a = jnp.arange(count_a, dtype=jnp.int32)
    index_b = jnp.arange(width, dtype=jnp.int32)
    angle_a = (
        2.0
        * math.pi
        / count_a
        * (index_a[:, None] * index_a[None, :] % count_a).astype(jnp.float32)
    )
    angle_b = (
        2.0 * math.pi / width * (index_b[:, None] * index_b[None, :] % width).astype(jnp.float32)
    )
    angle_t = (
        2.0 * math.pi / length * (index_a[:, None] * index_b[None, :] % length).astype(jnp.float32)
    )
    cos_a, sin_a = (jnp.cos(angle_a), jnp.sin(angle_a))
    cos_b, sin_b = (jnp.cos(angle_b), jnp.sin(angle_b))
    cos_t, sin_t = (jnp.cos(angle_t), jnp.sin(angle_t))
    wave = (index_a[:, None] + count_a * index_b[None, :]).astype(jnp.float32)
    symbol = base_kappa + base_conduct * (2.0 - 2.0 * jnp.cos(2.0 * math.pi * wave / length))
    factor = 1.0 / (symbol * symbol)
    highest = lax.Precision.HIGHEST
    section_real = jnp.einsum("pqab,ak->pqkb", shaped, cos_a, precision=highest)
    section_imag = -jnp.einsum("pqab,ak->pqkb", shaped, sin_a, precision=highest)
    twist_real = section_real * cos_t + section_imag * sin_t
    twist_imag = section_imag * cos_t - section_real * sin_t
    freq_real = (
        jnp.einsum("pqkb,bm->pqkm", twist_real, cos_b, precision=highest)
        + jnp.einsum("pqkb,bm->pqkm", twist_imag, sin_b, precision=highest)
    ) * factor
    freq_imag = (
        jnp.einsum("pqkb,bm->pqkm", twist_imag, cos_b, precision=highest)
        - jnp.einsum("pqkb,bm->pqkm", twist_real, sin_b, precision=highest)
    ) * factor
    back_real = jnp.einsum("pqkm,bm->pqkb", freq_real, cos_b, precision=highest) - jnp.einsum(
        "pqkm,bm->pqkb", freq_imag, sin_b, precision=highest
    )
    back_imag = jnp.einsum("pqkm,bm->pqkb", freq_imag, cos_b, precision=highest) + jnp.einsum(
        "pqkm,bm->pqkb", freq_real, sin_b, precision=highest
    )
    turn_real = back_real * cos_t - back_imag * sin_t
    turn_imag = back_imag * cos_t + back_real * sin_t
    result = jnp.einsum("pqkb,ak->pqab", turn_real, cos_a, precision=highest) - jnp.einsum(
        "pqkb,ak->pqab", turn_imag, sin_a, precision=highest
    )
    return (result / length).reshape(block.shape)


def precondition(residual):
    width = residual.shape[2]
    turned = spectral(
        lax.all_to_all(residual, "lon", split_axis=0, concat_axis=2, tiled=True), width
    )
    return lax.all_to_all(turned, "lon", split_axis=2, concat_axis=0, tiled=True)


def paired_sums(residual, precond, image):
    return lax.psum((jnp.sum(residual * precond), jnp.sum(image * precond)), ("lon", "lat"))


def body(noise, kappa2, conduct, land):
    levels, rows, columns = noise.shape
    width = 1
    ocean = land.astype(jnp.float32)
    row_global = lax.axis_index("lat") * rows + lax.broadcasted_iota(jnp.int32, (1, rows, 1), 1)
    total_rows = rows * lax.axis_size("lat")
    north_face = jnp.where(row_global < total_rows - 1, conduct[1], 0.0)
    level_index = lax.broadcasted_iota(jnp.int32, (levels, 1, 1), 0)
    upper_face = jnp.where(level_index < levels - 1, conduct[2], 0.0)
    statics = jnp.stack([kappa2, ocean, conduct[0], north_face, upper_face])
    west_column = shifted(conduct[0][:, :, columns - 1 :], "lon", 1)
    zero_column = jnp.zeros((5, levels, rows, 1), jnp.float32)
    low_column = zero_column.at[2].set(west_column)
    statics = jnp.concatenate([low_column, statics, zero_column], axis=3)
    south_row = shifted_2(statics[3][:, rows - 1 :, :], "lat", 1)
    zero_row = jnp.zeros((5, levels, 1, columns + 2), jnp.float32)
    low_row = zero_row.at[3].set(south_row)
    statics = jnp.concatenate([low_row, statics, zero_row], axis=2)
    solution = jnp.zeros_like(noise)
    residual = noise
    precond = precondition(residual)
    image = operator(precond, statics, width)
    energy, curvature = paired_sums(residual, precond, image)
    alpha = energy / curvature
    direction, along = (precond, image)
    for iteration in range(ITERS):
        solution = solution + alpha * direction
        residual = residual - alpha * along
        if iteration < ITERS - 1:
            precond = precondition(residual)
            image = operator(precond, statics, width)
            renewed, curvature = paired_sums(residual, precond, image)
            ratio = renewed / energy
            alpha = renewed / (curvature - ratio * renewed / alpha)
            direction = precond + ratio * direction
            along = image + ratio * along
            energy = renewed
    return (solution, residual)


def solution(mesh):
    return jax.shard_map(
        body,
        mesh=mesh,
        in_specs=(
            P("ens", "lat", "lon"),
            P(None, "lat", "lon"),
            P(None, None, "lat", "lon"),
            P(None, "lat", "lon"),
        ),
        out_specs=(P("ens", "lat", "lon"), P("ens", "lat", "lon")),
        check_vma=False,
    )
```

profile of v0, /device:TPU:0, one launch (start us, length us, event | category | flops | bytes accessed | tf_op | source)
XLA Modules:
  0.0 230.5 jit_solution(14411306132536024307)
XLA Ops:
  0.6 4.4 %all-to-all-start = ((f32[32,16,128]{2,1,0:T(8,128)}), f32[32,16,128]{2,1,0:T(8,128)S(1)}, u32[]{:S(2)}, u32[]{:S(2)}) async-start(f32[32,16,128]{2,1,0:T(8,128)} %param.8), calls=%async_computation | async-start | bytes 524288 | tf_op jit(solution)/shard_map/all_to_all | solution.py:132
  8.1 5.7 %collective-permute-done = f32[32,16,1]{2,1,0:T(8,128)S(1)} collective-permute-done((f32[32,16,1]{2,1,0:T(8,128)S(1)}, f32[32,16,1]{2,1,0:T(8,128)S(1)}, u32[]{:S(2)}, u32[]{:S(2)}) %collective-permute-start) | collective-permute-done | bytes 2080 | tf_op jit(solution)/shard_map/ppermute | solution.py:27
  15.9 4.1 %collective-permute-start.1 = (f32[32,1,130]{2,1,0:T(1,128)S(1)}, f32[32,1,130]{2,1,0:T(1,128)S(1)}, u32[]{:S(2)}, u32[]{:S(2)}) collective-permute-start(f32[32,1,130]{2,1,0:T(1,128)S(1)} %slice.336), channel_id=1, source_target_pairs={{0,1},{1,2},{2,3},{4,5},{5,6},{6,7},{8,9},{9,10},{10,11},{12,13},{... | collective-permute-start | bytes 49928 | tf_op jit(solution)/shard_map/ppermute | solution.py:33
  30.1 2.9 %reshape.184 = f32[4,1,16384]{2,1,0:T(1,128)} reshape(f32[512,8,16]{2,1,0:T(8,128)} %bitcast.172) | data formatting | bytes 524288
  33.0 3.6 %all-to-all-start.1 = ((f32[4,1,16384]{2,1,0:T(1,128)}), f32[4,1,16384]{2,1,0:T(1,128)S(1)}, u32[]{:S(2)}, u32[]{:S(2)}) async-start(f32[4,1,16384]{2,1,0:T(1,128)} %reshape.184), calls=%async_computation.1 | async-start | bytes 524288 | tf_op jit(solution)/shard_map/all_to_all | solution.py:134
  36.6 4.8 %fusion = f32[5,32,18,130]{3,2,1,0:T(8,128)} fusion(f32[1,32,1,130]{3,2,1,0:T(1,128)S(1)} %bitcast.182, f32[5,32,16,1]{3,2,1,0:T(8,128)S(1)} %broadcast_in_dim.29, f32[5,32,16,128]{3,2,1,0:T(8,128)} %copy-done.1, f32[5,32,16,1]{3,2,1,0:T(8,128)S(1)} %scatter.6, f32[18]{0:T(128)S(1)} %pad.79.clone), kind=kLoop, calls=%fused_computation.1 | loop fusion | flops 2246400 | bytes 2845512 | tf_op jit(solution)/shard_map/concatenate | solution.py:158
  47.8 2.2 slice_bitcast_fusion.3
  50.1 3.4 %collective-permute-done.3 = f32[32,16,1]{2,1,0:T(8,128)S(1)} collective-permute-done((f32[32,16,1]{2,1,0:T(8,128)S(1)}, f32[32,16,1]{2,1,0:T(8,128)S(1)}, u32[]{:S(2)}, u32[]{:S(2)}) %collective-permute-start.3) | collective-permute-done | bytes 2080 | tf_op jit(solution)/shard_map/ppermute | solution.py:19
  55.1 4.5 %collective-permute-start.5 = (f32[32,1,130]{2,1,0:T(1,128)S(1)}, f32[32,1,130]{2,1,0:T(1,128)S(1)}, u32[]{:S(2)}, u32[]{:S(2)}) collective-permute-start(f32[32,1,130]{2,1,0:T(1,128)S(1)} %get-tuple-element.51), channel_id=1, source_target_pairs={{0,1},{1,2},{2,3},{4,5},{5,6},{6,7},{8,9},{9,10},{10,11},{12,13},{... | collective-permute-start | bytes 49928 | tf_op jit(solution)/shard_map/ppermute | solution.py:19
  64.1 5.8 %collective-permute-done.7 = f32[32,16,1]{2,1,0:T(8,128)S(1)} collective-permute-done((f32[32,16,1]{2,1,0:T(8,128)S(1)}, f32[32,16,1]{2,1,0:T(8,128)S(1)}, u32[]{:S(2)}, u32[]{:S(2)}) %collective-permute-start.7) | collective-permute-done | bytes 2080 | tf_op jit(solution)/shard_map/ppermute | solution.py:19
  71.5 4.8 %collective-permute-start.9 = (f32[32,1,130]{2,1,0:T(1,128)S(1)}, f32[32,1,130]{2,1,0:T(1,128)S(1)}, u32[]{:S(2)}, u32[]{:S(2)}) collective-permute-start(f32[32,1,130]{2,1,0:T(1,128)S(1)} %get-tuple-element.47), channel_id=1, source_target_pairs={{0,1},{1,2},{2,3},{4,5},{5,6},{6,7},{8,9},{9,10},{10,11},{12,13},{... | collective-permute-start | bytes 49928 | tf_op jit(solution)/shard_map/ppermute | solution.py:19
  79.5 34.8 %all-reduce.12 = (f32[]{:T(128)}, f32[]{:T(128)}) all-reduce(f32[]{:T(128)} %get-tuple-element.31, f32[]{:T(128)} %get-tuple-element.30), channel_id=1, replica_groups=mesh['ens'=2,'lon'=4,'lat'=4] {'lon','lat'}, use_global_device_ids=true, to_apply=%region_1.2 | all-reduce | flops 2 | bytes 16 | tf_op jit(solution)/shard_map/psum | solution.py:138
  117.4 8.4 %all_to_all.66 = f32[32,16,128]{2,1,0:T(8,128)S(1)} all-to-all(f32[32,16,128]{2,1,0:T(8,128)S(1)} %multiply_subtract_fusion.2), channel_id=1, replica_groups=mesh['ens'=2,'lon'=4,'lat'=4] {'lon'}, dimensions={0} | all-to-all | bytes 524288 | tf_op jit(solution)/shard_map/all_to_all | solution.py:132
  135.8 2.3 reshape.186
  138.1 9.1 %all_to_all.67 = f32[4,1,16384]{2,1,0:T(1,128)} all-to-all(f32[4,1,16384]{2,1,0:T(1,128)S(1)} %reshape.186), channel_id=1, replica_groups=mesh['ens'=2,'lon'=4,'lat'=4] {'lon'}, dimensions={0} | all-to-all | bytes 524288 | tf_op jit(solution)/shard_map/all_to_all | solution.py:134
  147.2 2.3 reduce.5
  149.5 2.0 reshape.187
  151.5 2.9 %copy.138 = f32[8,16,4,128]{3,2,1,0:T(4,128)} copy(f32[8,16,4,128]{1,0,3,2:T(8,128)} %bitcast.175) | data formatting | bytes 524288 | tf_op jit(solution)/shard_map/all_to_all | solution.py:134
  157.3 6.2 %collective-permute-done.11 = f32[32,16,1]{2,1,0:T(8,128)S(1)} collective-permute-done((f32[32,16,1]{2,1,0:T(8,128)S(1)}, f32[32,16,1]{2,1,0:T(8,128)S(1)}, u32[]{:S(2)}, u32[]{:S(2)}) %collective-permute-start.11) | collective-permute-done | bytes 2080 | tf_op jit(solution)/shard_map/ppermute | solution.py:19
  165.1 4.5 %collective-permute-start.13 = (f32[32,1,130]{2,1,0:T(1,128)S(1)}, f32[32,1,130]{2,1,0:T(1,128)S(1)}, u32[]{:S(2)}, u32[]{:S(2)}) collective-permute-start(f32[32,1,130]{2,1,0:T(1,128)S(1)} %get-tuple-element.45), channel_id=1, source_target_pairs={{0,1},{1,2},{2,3},{4,5},{5,6},{6,7},{8,9},{9,10},{10,11},{12,13},{... | collective-permute-start | bytes 49928 | tf_op jit(solution)/shard_map/ppermute | solution.py:19
  174.0 6.3 %collective-permute-done.15 = f32[32,16,1]{2,1,0:T(8,128)S(1)} collective-permute-done((f32[32,16,1]{2,1,0:T(8,128)S(1)}, f32[32,16,1]{2,1,0:T(8,128)S(1)}, u32[]{:S(2)}, u32[]{:S(2)}) %collective-permute-start.15) | collective-permute-done | bytes 2080 | tf_op jit(solution)/shard_map/ppermute | solution.py:19
  181.9 4.9 %collective-permute-start.17 = (f32[32,1,130]{2,1,0:T(1,128)S(1)}, f32[32,1,130]{2,1,0:T(1,128)S(1)}, u32[]{:S(2)}, u32[]{:S(2)}) collective-permute-start(f32[32,1,130]{2,1,0:T(1,128)S(1)} %get-tuple-element.43), channel_id=1, source_target_pairs={{0,1},{1,2},{2,3},{4,5},{5,6},{6,7},{8,9},{9,10},{10,11},{12,13},{... | collective-permute-start | bytes 49928 | tf_op jit(solution)/shard_map/ppermute | solution.py:19
  188.4 2.3 fusion.73
  190.6 32.7 %all-reduce.11 = (f32[]{:T(128)}, f32[]{:T(128)}) all-reduce(f32[]{:T(128)} %get-tuple-element.29, f32[]{:T(128)} %get-tuple-element.28), channel_id=1, replica_groups=mesh['ens'=2,'lon'=4,'lat'=4] {'lon','lat'}, use_global_device_ids=true, to_apply=%region_5.6 | all-reduce | flops 2 | bytes 16 | tf_op jit(solution)/shard_map/psum | solution.py:138
  (119 shorter events, 58.5 us)
Async XLA Ops:
  0.6 19.3 %all-to-all-start = ((f32[32,16,128]{2,1,0:T(8,128)}), f32[32,16,128]{2,1,0:T(8,128)S(1)}, u32[]{:S(2)}, u32[]{:S(2)}) async-start(f32[32,16,128]{2,1,0:T(8,128)} %param.8), calls=%async_computation | async-start | bytes 524288 | tf_op jit(solution)/shard_map/all_to_all | solution.py:132
  7.2 6.7 %collective-permute-start = (f32[32,16,1]{2,1,0:T(8,128)S(1)}, f32[32,16,1]{2,1,0:T(8,128)S(1)}, u32[]{:S(2)}, u32[]{:S(2)}) collective-permute-start(f32[32,16,1]{2,1,0:T(8,128)S(1)} %slice.335), channel_id=1, source_target_pairs={{0,4},{4,8},{8,12},{12,0},{1,5},{5,9},{9,13},{13,1},{2,6},{6,10},{... | collective-permute-start | bytes 6152 | tf_op jit(solution)/shard_map/ppermute | solution.py:27
  15.9 20.7 %collective-permute-start.1 = (f32[32,1,130]{2,1,0:T(1,128)S(1)}, f32[32,1,130]{2,1,0:T(1,128)S(1)}, u32[]{:S(2)}, u32[]{:S(2)}) collective-permute-start(f32[32,1,130]{2,1,0:T(1,128)S(1)} %slice.336), channel_id=1, source_target_pairs={{0,1},{1,2},{2,3},{4,5},{5,6},{6,7},{8,9},{9,10},{10,11},{12,13},{... | collective-permute-start | bytes 49928 | tf_op jit(solution)/shard_map/ppermute | solution.py:33
  33.0 9.4 %all-to-all-start.1 = ((f32[4,1,16384]{2,1,0:T(1,128)}), f32[4,1,16384]{2,1,0:T(1,128)S(1)}, u32[]{:S(2)}, u32[]{:S(2)}) async-start(f32[4,1,16384]{2,1,0:T(1,128)} %reshape.184), calls=%async_computation.1 | async-start | bytes 524288 | tf_op jit(solution)/shard_map/all_to_all | solution.py:134
  46.0 7.5 %collective-permute-start.3 = (f32[32,16,1]{2,1,0:T(8,128)S(1)}, f32[32,16,1]{2,1,0:T(8,128)S(1)}, u32[]{:S(2)}, u32[]{:S(2)}) collective-permute-start(f32[32,16,1]{2,1,0:T(8,128)S(1)} %get-tuple-element.74), channel_id=1, source_target_pairs={{0,4},{4,8},{8,12},{12,0},{1,5},{5,9},{9,13},{13,1},{2,6},{6,10},{... | collective-permute-start | bytes 6152 | tf_op jit(solution)/shard_map/ppermute | solution.py:19
  46.1 7.4 %collective-permute-start.2 = (f32[32,16,1]{2,1,0:T(8,128)S(1)}, f32[32,16,1]{2,1,0:T(8,128)S(1)}, u32[]{:S(2)}, u32[]{:S(2)}) collective-permute-start(f32[32,16,1]{2,1,0:T(8,128)S(1)} %get-tuple-element.75), channel_id=1, source_target_pairs={{4,0},{8,4},{12,8},{0,12},{5,1},{9,5},{13,9},{1,13},{6,2},{10,6},{... | collective-permute-start | bytes 6152 | tf_op jit(solution)/shard_map/ppermute | solution.py:20
  50.0 28.0 %copy-start.3 = (f32[32,18,130]{2,1,0:T(8,128)}, f32[32,18,130]{2,1,0:T(8,128)S(1)}, u32[]{:S(2)}) copy-start(f32[32,18,130]{2,1,0:T(8,128)S(1)} %get-tuple-element.38) | copy-start | bytes 898564
  53.8 6.2 %collective-permute-start.4 = (f32[32,1,130]{2,1,0:T(1,128)S(1)}, f32[32,1,130]{2,1,0:T(1,128)S(1)}, u32[]{:S(2)}, u32[]{:S(2)}) collective-permute-start(f32[32,1,130]{2,1,0:T(1,128)S(1)} %get-tuple-element.50), channel_id=1, source_target_pairs={{1,0},{2,1},{3,2},{5,4},{6,5},{7,6},{9,8},{10,9},{11,10},{13,12},{... | collective-permute-start | bytes 49928 | tf_op jit(solution)/shard_map/ppermute | solution.py:20
  55.1 6.1 %collective-permute-start.5 = (f32[32,1,130]{2,1,0:T(1,128)S(1)}, f32[32,1,130]{2,1,0:T(1,128)S(1)}, u32[]{:S(2)}, u32[]{:S(2)}) collective-permute-start(f32[32,1,130]{2,1,0:T(1,128)S(1)} %get-tuple-element.51), channel_id=1, source_target_pairs={{0,1},{1,2},{2,3},{4,5},{5,6},{6,7},{8,9},{9,10},{10,11},{12,13},{... | collective-permute-start | bytes 49928 | tf_op jit(solution)/shard_map/ppermute | solution.py:19
  62.1 15.9 %copy-start.8 = (f32[32,16,128]{2,1,0:T(8,128)S(1)}, f32[32,16,128]{2,1,0:T(8,128)}, u32[]{:S(2)}) copy-start(f32[32,16,128]{2,1,0:T(8,128)} %param.8) | copy-start | bytes 786436
  62.3 7.6 %collective-permute-start.7 = (f32[32,16,1]{2,1,0:T(8,128)S(1)}, f32[32,16,1]{2,1,0:T(8,128)S(1)}, u32[]{:S(2)}, u32[]{:S(2)}) collective-permute-start(f32[32,16,1]{2,1,0:T(8,128)S(1)} %get-tuple-element.68), channel_id=1, source_target_pairs={{0,4},{4,8},{8,12},{12,0},{1,5},{5,9},{9,13},{13,1},{2,6},{6,10},{... | collective-permute-start | bytes 6152 | tf_op jit(solution)/shard_map/ppermute | solution.py:19
  62.3 7.6 %collective-permute-start.6 = (f32[32,16,1]{2,1,0:T(8,128)S(1)}, f32[32,16,1]{2,1,0:T(8,128)S(1)}, u32[]{:S(2)}, u32[]{:S(2)}) collective-permute-start(f32[32,16,1]{2,1,0:T(8,128)S(1)} %get-tuple-element.69), channel_id=1, source_target_pairs={{4,0},{8,4},{12,8},{0,12},{5,1},{9,5},{13,9},{1,13},{6,2},{10,6},{... | collective-permute-start | bytes 6152 | tf_op jit(solution)/shard_map/ppermute | solution.py:20
  70.2 6.2 %collective-permute-start.8 = (f32[32,1,130]{2,1,0:T(1,128)S(1)}, f32[32,1,130]{2,1,0:T(1,128)S(1)}, u32[]{:S(2)}, u32[]{:S(2)}) collective-permute-start(f32[32,1,130]{2,1,0:T(1,128)S(1)} %get-tuple-element.46), channel_id=1, source_target_pairs={{1,0},{2,1},{3,2},{5,4},{6,5},{7,6},{9,8},{10,9},{11,10},{13,12},{... | collective-permute-start | bytes 49928 | tf_op jit(solution)/shard_map/ppermute | solution.py:20
  71.5 6.6 %collective-permute-start.9 = (f32[32,1,130]{2,1,0:T(1,128)S(1)}, f32[32,1,130]{2,1,0:T(1,128)S(1)}, u32[]{:S(2)}, u32[]{:S(2)}) collective-permute-start(f32[32,1,130]{2,1,0:T(1,128)S(1)} %get-tuple-element.47), channel_id=1, source_target_pairs={{0,1},{1,2},{2,3},{4,5},{5,6},{6,7},{8,9},{9,10},{10,11},{12,13},{... | collective-permute-start | bytes 49928 | tf_op jit(solution)/shard_map/ppermute | solution.py:19
  79.5 48.0 %copy-start.7 = (f32[32,16,128]{2,1,0:T(8,128)}, f32[32,16,128]{2,1,0:T(8,128)S(1)}, u32[]{:S(2)}) copy-start(f32[32,16,128]{2,1,0:T(8,128)S(1)} %get-tuple-element.37) | copy-start | bytes 786436
  155.5 8.0 %collective-permute-start.11 = (f32[32,16,1]{2,1,0:T(8,128)S(1)}, f32[32,16,1]{2,1,0:T(8,128)S(1)}, u32[]{:S(2)}, u32[]{:S(2)}) collective-permute-start(f32[32,16,1]{2,1,0:T(8,128)S(1)} %get-tuple-element.66), channel_id=1, source_target_pairs={{0,4},{4,8},{8,12},{12,0},{1,5},{5,9},{9,13},{13,1},{2,6},{6,10},{... | collective-permute-start | bytes 6152 | tf_op jit(solution)/shard_map/ppermute | solution.py:19
  155.6 7.9 %collective-permute-start.10 = (f32[32,16,1]{2,1,0:T(8,128)S(1)}, f32[32,16,1]{2,1,0:T(8,128)S(1)}, u32[]{:S(2)}, u32[]{:S(2)}) collective-permute-start(f32[32,16,1]{2,1,0:T(8,128)S(1)} %get-tuple-element.67), channel_id=1, source_target_pairs={{4,0},{8,4},{12,8},{0,12},{5,1},{9,5},{13,9},{1,13},{6,2},{10,6},{... | collective-permute-start | bytes 6152 | tf_op jit(solution)/shard_map/ppermute | solution.py:20
  163.8 5.9 %collective-permute-start.12 = (f32[32,1,130]{2,1,0:T(1,128)S(1)}, f32[32,1,130]{2,1,0:T(1,128)S(1)}, u32[]{:S(2)}, u32[]{:S(2)}) collective-permute-start(f32[32,1,130]{2,1,0:T(1,128)S(1)} %get-tuple-element.44), channel_id=1, source_target_pairs={{1,0},{2,1},{3,2},{5,4},{6,5},{7,6},{9,8},{10,9},{11,10},{13,12},{... | collective-permute-start | bytes 49928 | tf_op jit(solution)/shard_map/ppermute | solution.py:20
  165.1 6.1 %collective-permute-start.13 = (f32[32,1,130]{2,1,0:T(1,128)S(1)}, f32[32,1,130]{2,1,0:T(1,128)S(1)}, u32[]{:S(2)}, u32[]{:S(2)}) collective-permute-start(f32[32,1,130]{2,1,0:T(1,128)S(1)} %get-tuple-element.45), channel_id=1, source_target_pairs={{0,1},{1,2},{2,3},{4,5},{5,6},{6,7},{8,9},{9,10},{10,11},{12,13},{... | collective-permute-start | bytes 49928 | tf_op jit(solution)/shard_map/ppermute | solution.py:19
  172.1 16.3 %copy-start.6 = (f32[32,16,128]{2,1,0:T(8,128)S(1)}, f32[32,16,128]{2,1,0:T(8,128)}, u32[]{:S(2)}) copy-start(f32[32,16,128]{2,1,0:T(8,128)} %copy-done.5) | copy-start | bytes 786436
  172.2 8.1 %collective-permute-start.15 = (f32[32,16,1]{2,1,0:T(8,128)S(1)}, f32[32,16,1]{2,1,0:T(8,128)S(1)}, u32[]{:S(2)}, u32[]{:S(2)}) collective-permute-start(f32[32,16,1]{2,1,0:T(8,128)S(1)} %get-tuple-element.60), channel_id=1, source_target_pairs={{0,4},{4,8},{8,12},{12,0},{1,5},{5,9},{9,13},{13,1},{2,6},{6,10},{... | collective-permute-start | bytes 6152 | tf_op jit(solution)/shard_map/ppermute | solution.py:19
  172.3 8.1 %collective-permute-start.14 = (f32[32,16,1]{2,1,0:T(8,128)S(1)}, f32[32,16,1]{2,1,0:T(8,128)S(1)}, u32[]{:S(2)}, u32[]{:S(2)}) collective-permute-start(f32[32,16,1]{2,1,0:T(8,128)S(1)} %get-tuple-element.61), channel_id=1, source_target_pairs={{4,0},{8,4},{12,8},{0,12},{5,1},{9,5},{13,9},{1,13},{6,2},{10,6},{... | collective-permute-start | bytes 6152 | tf_op jit(solution)/shard_map/ppermute | solution.py:20
  180.6 6.2 %collective-permute-start.16 = (f32[32,1,130]{2,1,0:T(1,128)S(1)}, f32[32,1,130]{2,1,0:T(1,128)S(1)}, u32[]{:S(2)}, u32[]{:S(2)}) collective-permute-start(f32[32,1,130]{2,1,0:T(1,128)S(1)} %get-tuple-element.42), channel_id=1, source_target_pairs={{1,0},{2,1},{3,2},{5,4},{6,5},{7,6},{9,8},{10,9},{11,10},{13,12},{... | collective-permute-start | bytes 49928 | tf_op jit(solution)/shard_map/ppermute | solution.py:20
  181.9 6.4 %collective-permute-start.17 = (f32[32,1,130]{2,1,0:T(1,128)S(1)}, f32[32,1,130]{2,1,0:T(1,128)S(1)}, u32[]{:S(2)}, u32[]{:S(2)}) collective-permute-start(f32[32,1,130]{2,1,0:T(1,128)S(1)} %get-tuple-element.43), channel_id=1, source_target_pairs={{0,1},{1,2},{2,3},{4,5},{5,6},{6,7},{8,9},{9,10},{10,11},{12,13},{... | collective-permute-start | bytes 49928 | tf_op jit(solution)/shard_map/ppermute | solution.py:19
  (6 other events, 31.2 us)
where the time goes:
time: 232 us; the launch traced here: 231 us
  blocking collectives  84.9 us (37%)
  starting transfers between devices  43.7 us (19%)
  waiting for transfers between devices  34.7 us (15%)
  local copies, waits for them, and re-layouts  23.7 us (10%)
  other arithmetic  20.2 us (9%)
  matrix products  16 us (7%)
  between operations  7.26 us (3%)
    psum x2, blocking collectives, paired_sums(): lax.psum((jnp.sum(residual * precond), jnp.sum(image * precond)), ('lon',...  67.5 us
    ppermute x8, waiting for transfers between devices, padded_2(): before = lax.ppermute(last, axis, up)  27.8 us
    ppermute x8, starting transfers between devices, padded_2(): before = lax.ppermute(last, axis, up)  19 us
    ppermute x8, starting transfers between devices, padded_2(): after = lax.ppermute(initial, axis, down)  12.1 us
    unnamed x25, local copies, waits for them, and re-layouts  10.9 us
    all_to_all x1, blocking collectives, precondition(): lax.all_to_all(turned, 'lon', split_axis=2, concat_axis=0, tiled=True)  9.07 us
    all_to_all x1, blocking collectives, precondition(): lax.all_to_all(residual, 'lon', split_axis=0, concat_axis=2, tiled=True)  8.38 us
    ppermute x1, waiting for transfers between devices, shifted(): return lax.ppermute(x, axis, [(i, (i + by) % size) for i in range(size)])  5.71 us
  transfers between devices with their start and end apart: 20, of which 11 were waited for; matrix products, arithmetic and copies ran while one was open for 10% of the time, Pallas kernels for 0%

commit v1 on v0

--- a/solution.py
+++ b/solution.py
@@ -131,7 +131,10 @@
     turned = spectral(
         lax.all_to_all(residual, "lon", split_axis=0, concat_axis=2, tiled=True), width
     )
-    return lax.all_to_all(turned, "lon", split_axis=2, concat_axis=0, tiled=True)
+    return jnp.concatenate(
+        lax.all_to_all(jnp.stack(jnp.split(turned, lax.axis_size("lon"), axis=2)), "lon", 0, 0),
+        axis=0,
+    )
 
 
 def paired_sums(residual, precond, image):

time: 232 us -> 213 us (0.918)
  local copies, waits for them, and re-layouts: 23.7 us -> 8.93 us
  other arithmetic: 20.2 us -> 17.5 us
    unnamed x25, local copies, waits for them, and re-layouts: 10.9 us -> 3.26 us
    all_to_all x5 -> x0, local copies, waits for them, and re-layouts: 5.07 us -> none  [precondition(): lax.all_to_all(turned, 'lon', split_axis=2, concat_axis=0, tiled=True)]
    all_to_all x2 -> x0, other arithmetic: 3.65 us -> none  [precondition(): lax.all_to_all(turned, 'lon', split_axis=2, concat_axis=0, tiled=True)]
    reshape x2, local copies, waits for them, and re-layouts: 3.93 us -> 0.91 us  [spectral(): return (result / length).reshape(block.shape)]
  transfers between devices with their start and end apart: 20 -> 20, of which waited for: 11 -> 11; matrix products, arithmetic and copies ran while one was open for 10% -> 9% of each run, Pallas kernels for 0% -> 0%
where the time goes in v1:
time: 213 us; the launch traced here: 212 us
  blocking collectives  84.5 us (40%)
  starting transfers between devices  43.2 us (20%)
  waiting for transfers between devices  34.7 us (16%)
  other arithmetic  17.5 us (8%)
  matrix products  16 us (8%)
  local copies, waits for them, and re-layouts  8.93 us (4%)
  between operations  7.03 us (3%)
    psum x2, blocking collectives, paired_sums(): lax.psum((jnp.sum(residual * precond), jnp.sum(image * precond)), ('lon',...  67.7 us
    ppermute x8, waiting for transfers between devices, padded_2(): before = lax.ppermute(last, axis, up)  27.7 us
    ppermute x8, starting transfers between devices, padded_2(): before = lax.ppermute(last, axis, up)  19.1 us
    ppermute x8, starting transfers between devices, padded_2(): after = lax.ppermute(initial, axis, down)  11.6 us
    all_to_all x1, blocking collectives, precondition(): lax.all_to_all(jnp.stack(jnp.split(turned, lax.axis_size('lon'), axis=2))...  8.39 us
    all_to_all x1, blocking collectives, precondition(): lax.all_to_all(residual, 'lon', split_axis=0, concat_axis=2, tiled=True)  8.38 us
    ppermute x1, waiting for transfers between devices, shifted(): return lax.ppermute(x, axis, [(i, (i + by) % size) for i in range(size)])  5.71 us
    concatenate x1, other arithmetic, body(): statics = jnp.concatenate([low_row, statics, zero_row], axis=2)  4.86 us
  transfers between devices with their start and end apart: 20, of which 11 were waited for; matrix products, arithmetic and copies ran while one was open for 9% of the time, Pallas kernels for 0%

profile of v1, /device:TPU:0, one launch (start us, length us, event | category | flops | bytes accessed | tf_op | source)
XLA Modules:
  0.0 211.9 jit_solution(16148635258922694993)
XLA Ops:
  0.6 4.4 %all-to-all-start = ((f32[32,16,128]{2,1,0:T(8,128)}), f32[32,16,128]{2,1,0:T(8,128)S(1)}, u32[]{:S(2)}, u32[]{:S(2)}) async-start(f32[32,16,128]{2,1,0:T(8,128)} %param.8), calls=%async_computation | async-start | bytes 524288 | tf_op jit(solution)/shard_map/all_to_all | solution.py:132
  8.1 5.7 %collective-permute-done = f32[32,16,1]{2,1,0:T(8,128)S(1)} collective-permute-done((f32[32,16,1]{2,1,0:T(8,128)S(1)}, f32[32,16,1]{2,1,0:T(8,128)S(1)}, u32[]{:S(2)}, u32[]{:S(2)}) %collective-permute-start) | collective-permute-done | bytes 2080 | tf_op jit(solution)/shard_map/ppermute | solution.py:27
  15.9 4.1 %collective-permute-start.1 = (f32[32,1,130]{2,1,0:T(1,128)S(1)}, f32[32,1,130]{2,1,0:T(1,128)S(1)}, u32[]{:S(2)}, u32[]{:S(2)}) collective-permute-start(f32[32,1,130]{2,1,0:T(1,128)S(1)} %slice.336), channel_id=1, source_target_pairs={{0,1},{1,2},{2,3},{4,5},{5,6},{6,7},{8,9},{9,10},{10,11},{12,13},{... | collective-permute-start | bytes 49928 | tf_op jit(solution)/shard_map/ppermute | solution.py:33
  28.9 3.4 %all-to-all-start.1 = ((f32[4,8,16,128]{3,2,1,0:T(8,128)}), f32[4,8,16,128]{3,2,1,0:T(8,128)S(1)}, u32[]{:S(2)}, u32[]{:S(2)}) async-start(f32[4,8,16,128]{3,2,1,0:T(8,128)} %pad_maximum_fusion.34), calls=%async_computation.1 | async-start | bytes 524288 | tf_op jit(solution)/shard_map/all_to_all | solution.py:135
  32.4 4.9 %fusion = f32[5,32,18,130]{3,2,1,0:T(8,128)} fusion(f32[1,32,1,130]{3,2,1,0:T(1,128)S(1)} %bitcast.182, f32[5,32,16,1]{3,2,1,0:T(8,128)S(1)} %broadcast_in_dim.29, f32[5,32,16,128]{3,2,1,0:T(8,128)} %copy-done.1, f32[5,32,16,1]{3,2,1,0:T(8,128)S(1)} %scatter.6, f32[18]{0:T(128)S(1)} %pad.83.clone), kind=kLoop, calls=%fused_computation.1 | loop fusion | flops 2246400 | bytes 2845512 | tf_op jit(solution)/shard_map/concatenate | solution.py:161
  40.3 2.1 %slice_bitcast_fusion.3 = (f32[32,18,130]{2,1,0:T(8,128)S(1)}, f32[32,18,130]{2,1,0:T(8,128)S(1)}, f32[32,18,130]{2,1,0:T(8,128)S(1)}, f32[32,18,130]{2,1,0:T(8,128)S(1)}) fusion(f32[5,32,18,130]{3,2,1,0:T(8,128)} %fusion), kind=kLoop, calls=%fused_computation.26 | loop fusion | bytes 2396160 | tf_op jit(solution)/shard_map/squeeze | solution.py:43
  42.6 3.4 %collective-permute-done.3 = f32[32,16,1]{2,1,0:T(8,128)S(1)} collective-permute-done((f32[32,16,1]{2,1,0:T(8,128)S(1)}, f32[32,16,1]{2,1,0:T(8,128)S(1)}, u32[]{:S(2)}, u32[]{:S(2)}) %collective-permute-start.3) | collective-permute-done | bytes 2080 | tf_op jit(solution)/shard_map/ppermute | solution.py:19
  47.6 4.5 %collective-permute-start.5 = (f32[32,1,130]{2,1,0:T(1,128)S(1)}, f32[32,1,130]{2,1,0:T(1,128)S(1)}, u32[]{:S(2)}, u32[]{:S(2)}) collective-permute-start(f32[32,1,130]{2,1,0:T(1,128)S(1)} %get-tuple-element.51), channel_id=1, source_target_pairs={{0,1},{1,2},{2,3},{4,5},{5,6},{6,7},{8,9},{9,10},{10,11},{12,13},{... | collective-permute-start | bytes 49928 | tf_op jit(solution)/shard_map/ppermute | solution.py:19
  54.8 1.7 collective-permute-start.6
  56.6 5.7 %collective-permute-done.7 = f32[32,16,1]{2,1,0:T(8,128)S(1)} collective-permute-done((f32[32,16,1]{2,1,0:T(8,128)S(1)}, f32[32,16,1]{2,1,0:T(8,128)S(1)}, u32[]{:S(2)}, u32[]{:S(2)}) %collective-permute-start.7) | collective-permute-done | bytes 2080 | tf_op jit(solution)/shard_map/ppermute | solution.py:19
  63.9 4.9 %collective-permute-start.9 = (f32[32,1,130]{2,1,0:T(1,128)S(1)}, f32[32,1,130]{2,1,0:T(1,128)S(1)}, u32[]{:S(2)}, u32[]{:S(2)}) collective-permute-start(f32[32,1,130]{2,1,0:T(1,128)S(1)} %get-tuple-element.47), channel_id=1, source_target_pairs={{0,1},{1,2},{2,3},{4,5},{5,6},{6,7},{8,9},{9,10},{10,11},{12,13},{... | collective-permute-start | bytes 49928 | tf_op jit(solution)/shard_map/ppermute | solution.py:19
  68.9 1.7 collective-permute-done.9
  72.1 35.1 %all-reduce.12 = (f32[]{:T(128)}, f32[]{:T(128)}) all-reduce(f32[]{:T(128)} %get-tuple-element.31, f32[]{:T(128)} %get-tuple-element.30), channel_id=1, replica_groups=mesh['ens'=2,'lon'=4,'lat'=4] {'lon','lat'}, use_global_device_ids=true, to_apply=%region_1.2 | all-reduce | flops 2 | bytes 16 | tf_op jit(solution)/shard_map/psum | solution.py:141
  110.1 8.4 %all_to_all.40 = f32[32,16,128]{2,1,0:T(8,128)S(1)} all-to-all(f32[32,16,128]{2,1,0:T(8,128)S(1)} %multiply_subtract_fusion.2), channel_id=1, replica_groups=mesh['ens'=2,'lon'=4,'lat'=4] {'lon'}, dimensions={0} | all-to-all | bytes 524288 | tf_op jit(solution)/shard_map/all_to_all | solution.py:132
  128.5 8.4 %all_to_all.41 = f32[4,8,16,128]{3,2,1,0:T(8,128)S(1)} all-to-all(f32[4,8,16,128]{3,2,1,0:T(8,128)S(1)} %pad_maximum_fusion.35), channel_id=1, replica_groups=mesh['ens'=2,'lon'=4,'lat'=4] {'lon'}, dimensions={0} | all-to-all | bytes 524288 | tf_op jit(solution)/shard_map/all_to_all | solution.py:135
  137.1 1.7 collective-permute-start.10
  138.8 6.2 %collective-permute-done.11 = f32[32,16,1]{2,1,0:T(8,128)S(1)} collective-permute-done((f32[32,16,1]{2,1,0:T(8,128)S(1)}, f32[32,16,1]{2,1,0:T(8,128)S(1)}, u32[]{:S(2)}, u32[]{:S(2)}) %collective-permute-start.11) | collective-permute-done | bytes 2080 | tf_op jit(solution)/shard_map/ppermute | solution.py:19
  146.6 4.5 %collective-permute-start.13 = (f32[32,1,130]{2,1,0:T(1,128)S(1)}, f32[32,1,130]{2,1,0:T(1,128)S(1)}, u32[]{:S(2)}, u32[]{:S(2)}) collective-permute-start(f32[32,1,130]{2,1,0:T(1,128)S(1)} %get-tuple-element.45), channel_id=1, source_target_pairs={{0,1},{1,2},{2,3},{4,5},{5,6},{6,7},{8,9},{9,10},{10,11},{12,13},{... | collective-permute-start | bytes 49928 | tf_op jit(solution)/shard_map/ppermute | solution.py:19
  153.9 1.7 collective-permute-start.14
  155.6 6.3 %collective-permute-done.15 = f32[32,16,1]{2,1,0:T(8,128)S(1)} collective-permute-done((f32[32,16,1]{2,1,0:T(8,128)S(1)}, f32[32,16,1]{2,1,0:T(8,128)S(1)}, u32[]{:S(2)}, u32[]{:S(2)}) %collective-permute-start.15) | collective-permute-done | bytes 2080 | tf_op jit(solution)/shard_map/ppermute | solution.py:19
  163.5 4.9 %collective-permute-start.17 = (f32[32,1,130]{2,1,0:T(1,128)S(1)}, f32[32,1,130]{2,1,0:T(1,128)S(1)}, u32[]{:S(2)}, u32[]{:S(2)}) collective-permute-start(f32[32,1,130]{2,1,0:T(1,128)S(1)} %get-tuple-element.43), channel_id=1, source_target_pairs={{0,1},{1,2},{2,3},{4,5},{5,6},{6,7},{8,9},{9,10},{10,11},{12,13},{... | collective-permute-start | bytes 49928 | tf_op jit(solution)/shard_map/ppermute | solution.py:19
  169.9 2.2 %fusion.73 = (f32[]{:T(128)}, f32[]{:T(128)}, f32[32,16,128]{2,1,0:T(8,128)}) fusion(f32[4,8,16,128]{3,2,1,0:T(8,128)S(1)} %all_to_all.41, f32[32,16,128]{2,1,0:T(8,128)S(1)} %copy-done.8, f32[32,16,128]{2,1,0:T(8,128)S(1)} %fusion.31, f32[31,16,128]{2,1,0:T(8,128)S(1)} %get-tuple-element.63, f32[31,16,128]{2,1,0:T(8,128)S(1)} %slice.350, ...), kind=kLoop, calls=%fused_computation.132 | loop fusion | flops 2359294 | bytes 3682824 | tf_op jit(solution)/shard_map/reduce_sum | solution.py:141
  172.2 32.6 %all-reduce.11 = (f32[]{:T(128)}, f32[]{:T(128)}) all-reduce(f32[]{:T(128)} %get-tuple-element.29, f32[]{:T(128)} %get-tuple-element.28), channel_id=1, replica_groups=mesh['ens'=2,'lon'=4,'lat'=4] {'lon','lat'}, use_global_device_ids=true, to_apply=%region_5.6 | all-reduce | flops 2 | bytes 16 | tf_op jit(solution)/shard_map/psum | solution.py:141
  209.3 1.9 multiply_subtract_fusion
  (116 shorter events, 44.3 us)
Async XLA Ops:
  0.6 19.3 %all-to-all-start = ((f32[32,16,128]{2,1,0:T(8,128)}), f32[32,16,128]{2,1,0:T(8,128)S(1)}, u32[]{:S(2)}, u32[]{:S(2)}) async-start(f32[32,16,128]{2,1,0:T(8,128)} %param.8), calls=%async_computation | async-start | bytes 524288 | tf_op jit(solution)/shard_map/all_to_all | solution.py:132
  7.2 6.7 %collective-permute-start = (f32[32,16,1]{2,1,0:T(8,128)S(1)}, f32[32,16,1]{2,1,0:T(8,128)S(1)}, u32[]{:S(2)}, u32[]{:S(2)}) collective-permute-start(f32[32,16,1]{2,1,0:T(8,128)S(1)} %slice.335), channel_id=1, source_target_pairs={{0,4},{4,8},{8,12},{12,0},{1,5},{5,9},{9,13},{13,1},{2,6},{6,10},{... | collective-permute-start | bytes 6152 | tf_op jit(solution)/shard_map/ppermute | solution.py:27
  15.9 16.5 %collective-permute-start.1 = (f32[32,1,130]{2,1,0:T(1,128)S(1)}, f32[32,1,130]{2,1,0:T(1,128)S(1)}, u32[]{:S(2)}, u32[]{:S(2)}) collective-permute-start(f32[32,1,130]{2,1,0:T(1,128)S(1)} %slice.336), channel_id=1, source_target_pairs={{0,1},{1,2},{2,3},{4,5},{5,6},{6,7},{8,9},{9,10},{10,11},{12,13},{... | collective-permute-start | bytes 49928 | tf_op jit(solution)/shard_map/ppermute | solution.py:33
  28.9 9.4 %all-to-all-start.1 = ((f32[4,8,16,128]{3,2,1,0:T(8,128)}), f32[4,8,16,128]{3,2,1,0:T(8,128)S(1)}, u32[]{:S(2)}, u32[]{:S(2)}) async-start(f32[4,8,16,128]{3,2,1,0:T(8,128)} %pad_maximum_fusion.34), calls=%async_computation.1 | async-start | bytes 524288 | tf_op jit(solution)/shard_map/all_to_all | solution.py:135
  38.5 7.5 %collective-permute-start.3 = (f32[32,16,1]{2,1,0:T(8,128)S(1)}, f32[32,16,1]{2,1,0:T(8,128)S(1)}, u32[]{:S(2)}, u32[]{:S(2)}) collective-permute-start(f32[32,16,1]{2,1,0:T(8,128)S(1)} %get-tuple-element.78), channel_id=1, source_target_pairs={{0,4},{4,8},{8,12},{12,0},{1,5},{5,9},{9,13},{13,1},{2,6},{6,10},{... | collective-permute-start | bytes 6152 | tf_op jit(solution)/shard_map/ppermute | solution.py:19
  39.0 7.0 %collective-permute-start.2 = (f32[32,16,1]{2,1,0:T(8,128)S(1)}, f32[32,16,1]{2,1,0:T(8,128)S(1)}, u32[]{:S(2)}, u32[]{:S(2)}) collective-permute-start(f32[32,16,1]{2,1,0:T(8,128)S(1)} %get-tuple-element.79), channel_id=1, source_target_pairs={{4,0},{8,4},{12,8},{0,12},{5,1},{9,5},{13,9},{1,13},{6,2},{10,6},{... | collective-permute-start | bytes 6152 | tf_op jit(solution)/shard_map/ppermute | solution.py:20
  42.5 28.1 %copy-start.3 = (f32[32,18,130]{2,1,0:T(8,128)}, f32[32,18,130]{2,1,0:T(8,128)S(1)}, u32[]{:S(2)}) copy-start(f32[32,18,130]{2,1,0:T(8,128)S(1)} %get-tuple-element.38) | copy-start | bytes 898564
  46.3 6.1 %collective-permute-start.4 = (f32[32,1,130]{2,1,0:T(1,128)S(1)}, f32[32,1,130]{2,1,0:T(1,128)S(1)}, u32[]{:S(2)}, u32[]{:S(2)}) collective-permute-start(f32[32,1,130]{2,1,0:T(1,128)S(1)} %get-tuple-element.50), channel_id=1, source_target_pairs={{1,0},{2,1},{3,2},{5,4},{6,5},{7,6},{9,8},{10,9},{11,10},{13,12},{... | collective-permute-start | bytes 49928 | tf_op jit(solution)/shard_map/ppermute | solution.py:20
  47.6 6.1 %collective-permute-start.5 = (f32[32,1,130]{2,1,0:T(1,128)S(1)}, f32[32,1,130]{2,1,0:T(1,128)S(1)}, u32[]{:S(2)}, u32[]{:S(2)}) collective-permute-start(f32[32,1,130]{2,1,0:T(1,128)S(1)} %get-tuple-element.51), channel_id=1, source_target_pairs={{0,1},{1,2},{2,3},{4,5},{5,6},{6,7},{8,9},{9,10},{10,11},{12,13},{... | collective-permute-start | bytes 49928 | tf_op jit(solution)/shard_map/ppermute | solution.py:19
  54.6 15.9 %copy-start.6 = (f32[4,8,16,128]{3,2,1,0:T(8,128)S(1)}, f32[4,8,16,128]{3,2,1,0:T(8,128)}, u32[]{:S(2)}) copy-start(f32[4,8,16,128]{3,2,1,0:T(8,128)} %copy-done.5) | copy-start | bytes 786436
  54.8 7.5 %collective-permute-start.7 = (f32[32,16,1]{2,1,0:T(8,128)S(1)}, f32[32,16,1]{2,1,0:T(8,128)S(1)}, u32[]{:S(2)}, u32[]{:S(2)}) collective-permute-start(f32[32,16,1]{2,1,0:T(8,128)S(1)} %get-tuple-element.72), channel_id=1, source_target_pairs={{0,4},{4,8},{8,12},{12,0},{1,5},{5,9},{9,13},{13,1},{2,6},{6,10},{... | collective-permute-start | bytes 6152 | tf_op jit(solution)/shard_map/ppermute | solution.py:19
  54.8 7.5 %collective-permute-start.6 = (f32[32,16,1]{2,1,0:T(8,128)S(1)}, f32[32,16,1]{2,1,0:T(8,128)S(1)}, u32[]{:S(2)}, u32[]{:S(2)}) collective-permute-start(f32[32,16,1]{2,1,0:T(8,128)S(1)} %get-tuple-element.73), channel_id=1, source_target_pairs={{4,0},{8,4},{12,8},{0,12},{5,1},{9,5},{13,9},{1,13},{6,2},{10,6},{... | collective-permute-start | bytes 6152 | tf_op jit(solution)/shard_map/ppermute | solution.py:20
  62.6 6.2 %collective-permute-start.8 = (f32[32,1,130]{2,1,0:T(1,128)S(1)}, f32[32,1,130]{2,1,0:T(1,128)S(1)}, u32[]{:S(2)}, u32[]{:S(2)}) collective-permute-start(f32[32,1,130]{2,1,0:T(1,128)S(1)} %get-tuple-element.46), channel_id=1, source_target_pairs={{1,0},{2,1},{3,2},{5,4},{6,5},{7,6},{9,8},{10,9},{11,10},{13,12},{... | collective-permute-start | bytes 49928 | tf_op jit(solution)/shard_map/ppermute | solution.py:20
  63.9 6.6 %collective-permute-start.9 = (f32[32,1,130]{2,1,0:T(1,128)S(1)}, f32[32,1,130]{2,1,0:T(1,128)S(1)}, u32[]{:S(2)}, u32[]{:S(2)}) collective-permute-start(f32[32,1,130]{2,1,0:T(1,128)S(1)} %get-tuple-element.47), channel_id=1, source_target_pairs={{0,1},{1,2},{2,3},{4,5},{5,6},{6,7},{8,9},{9,10},{10,11},{12,13},{... | collective-permute-start | bytes 49928 | tf_op jit(solution)/shard_map/ppermute | solution.py:19
  72.1 48.3 %copy-start.9 = (f32[32,16,128]{2,1,0:T(8,128)}, f32[32,16,128]{2,1,0:T(8,128)S(1)}, u32[]{:S(2)}) copy-start(f32[32,16,128]{2,1,0:T(8,128)S(1)} %get-tuple-element.37) | copy-start | bytes 786436
  137.0 8.0 %collective-permute-start.11 = (f32[32,16,1]{2,1,0:T(8,128)S(1)}, f32[32,16,1]{2,1,0:T(8,128)S(1)}, u32[]{:S(2)}, u32[]{:S(2)}) collective-permute-start(f32[32,16,1]{2,1,0:T(8,128)S(1)} %get-tuple-element.66), channel_id=1, source_target_pairs={{0,4},{4,8},{8,12},{12,0},{1,5},{5,9},{9,13},{13,1},{2,6},{6,10},{... | collective-permute-start | bytes 6152 | tf_op jit(solution)/shard_map/ppermute | solution.py:19
  137.1 7.9 %collective-permute-start.10 = (f32[32,16,1]{2,1,0:T(8,128)S(1)}, f32[32,16,1]{2,1,0:T(8,128)S(1)}, u32[]{:S(2)}, u32[]{:S(2)}) collective-permute-start(f32[32,16,1]{2,1,0:T(8,128)S(1)} %get-tuple-element.67), channel_id=1, source_target_pairs={{4,0},{8,4},{12,8},{0,12},{5,1},{9,5},{13,9},{1,13},{6,2},{10,6},{... | collective-permute-start | bytes 6152 | tf_op jit(solution)/shard_map/ppermute | solution.py:20
  145.3 5.9 %collective-permute-start.12 = (f32[32,1,130]{2,1,0:T(1,128)S(1)}, f32[32,1,130]{2,1,0:T(1,128)S(1)}, u32[]{:S(2)}, u32[]{:S(2)}) collective-permute-start(f32[32,1,130]{2,1,0:T(1,128)S(1)} %get-tuple-element.44), channel_id=1, source_target_pairs={{1,0},{2,1},{3,2},{5,4},{6,5},{7,6},{9,8},{10,9},{11,10},{13,12},{... | collective-permute-start | bytes 49928 | tf_op jit(solution)/shard_map/ppermute | solution.py:20
  146.6 6.1 %collective-permute-start.13 = (f32[32,1,130]{2,1,0:T(1,128)S(1)}, f32[32,1,130]{2,1,0:T(1,128)S(1)}, u32[]{:S(2)}, u32[]{:S(2)}) collective-permute-start(f32[32,1,130]{2,1,0:T(1,128)S(1)} %get-tuple-element.45), channel_id=1, source_target_pairs={{0,1},{1,2},{2,3},{4,5},{5,6},{6,7},{8,9},{9,10},{10,11},{12,13},{... | collective-permute-start | bytes 49928 | tf_op jit(solution)/shard_map/ppermute | solution.py:19
  153.6 16.3 %copy-start.8 = (f32[32,16,128]{2,1,0:T(8,128)S(1)}, f32[32,16,128]{2,1,0:T(8,128)}, u32[]{:S(2)}) copy-start(f32[32,16,128]{2,1,0:T(8,128)} %copy-done.7) | copy-start | bytes 786436
  153.8 8.1 %collective-permute-start.15 = (f32[32,16,1]{2,1,0:T(8,128)S(1)}, f32[32,16,1]{2,1,0:T(8,128)S(1)}, u32[]{:S(2)}, u32[]{:S(2)}) collective-permute-start(f32[32,16,1]{2,1,0:T(8,128)S(1)} %get-tuple-element.60), channel_id=1, source_target_pairs={{0,4},{4,8},{8,12},{12,0},{1,5},{5,9},{9,13},{13,1},{2,6},{6,10},{... | collective-permute-start | bytes 6152 | tf_op jit(solution)/shard_map/ppermute | solution.py:19
  153.9 8.1 %collective-permute-start.14 = (f32[32,16,1]{2,1,0:T(8,128)S(1)}, f32[32,16,1]{2,1,0:T(8,128)S(1)}, u32[]{:S(2)}, u32[]{:S(2)}) collective-permute-start(f32[32,16,1]{2,1,0:T(8,128)S(1)} %get-tuple-element.61), channel_id=1, source_target_pairs={{4,0},{8,4},{12,8},{0,12},{5,1},{9,5},{13,9},{1,13},{6,2},{10,6},{... | collective-permute-start | bytes 6152 | tf_op jit(solution)/shard_map/ppermute | solution.py:20
  162.2 6.2 %collective-permute-start.16 = (f32[32,1,130]{2,1,0:T(1,128)S(1)}, f32[32,1,130]{2,1,0:T(1,128)S(1)}, u32[]{:S(2)}, u32[]{:S(2)}) collective-permute-start(f32[32,1,130]{2,1,0:T(1,128)S(1)} %get-tuple-element.42), channel_id=1, source_target_pairs={{1,0},{2,1},{3,2},{5,4},{6,5},{7,6},{9,8},{10,9},{11,10},{13,12},{... | collective-permute-start | bytes 49928 | tf_op jit(solution)/shard_map/ppermute | solution.py:20
  163.5 6.4 %collective-permute-start.17 = (f32[32,1,130]{2,1,0:T(1,128)S(1)}, f32[32,1,130]{2,1,0:T(1,128)S(1)}, u32[]{:S(2)}, u32[]{:S(2)}) collective-permute-start(f32[32,1,130]{2,1,0:T(1,128)S(1)} %get-tuple-element.43), channel_id=1, source_target_pairs={{0,1},{1,2},{2,3},{4,5},{5,6},{6,7},{8,9},{9,10},{10,11},{12,13},{... | collective-permute-start | bytes 49928 | tf_op jit(solution)/shard_map/ppermute | solution.py:19
  (8 other events, 52.8 us)
